TPU v7x, 32 devices: a whole 2x2x4 slice. The times are simulated.
32 devices in a mesh: space: 4 (over x, core), mem: 8 (over z, y).
Axes of the slice: x: 2, y: 2, z: 4, core: 2. Of those that a mesh axis runs over, the one named last changes fastest.
Arguments:
- prior_ensemble: float32 [512, 8192], P('mem', 'space'), may hold values from -5 to 5
- terminal_particles: float32 [512, 8192], P(None, ('space', 'mem')), may hold values from -5 to 5
- reverse_perturbation: float32 [3, 512, 8192], P(None, None, ('space', 'mem')), may hold values from -6 to 6
- measured_angles: float32 [8192], P(('space', 'mem')), may hold values from -1.3 to 1.3
Outputs:
- analysis: float32 [512, 8192], P(None, ('space', 'mem'))
All inputs are finite; a program needn't handle non-finite values.
Results may differ from a plain program's by a relative error of at most 0.0003.
Values sent between devices are 32-bit elements; how exact they have to be, the bound alone decides.
A program may use at most 64 MiB of HBM per device.

v0:
```python
import math
import jax
import jax.numpy as jnp
from jax import lax
from jax.sharding import PartitionSpec as P

ITERS = 3


def member_weights(inner_pairing_matrix, particle_lengths, alpha, sigma2, temper):
    logits = (2.0 * alpha * inner_pairing_matrix - alpha * alpha * particle_lengths[None, :]) / (
        2.0 * sigma2 * temper
    )
    return jax.nn.softmax(logits, axis=1)


def per_device(prior_ensemble, terminal_particles, reverse_perturbation, measured_angles):
    peak_log_likelihood = lax.Precision.HIGHEST
    particle_vectors = lax.all_to_all(
        prior_ensemble, "mem", split_axis=1, concat_axis=0, tiled=True
    )
    devices_all = lax.axis_size("space") * lax.axis_size("mem")
    temper = math.sqrt(particle_vectors.shape[1] * devices_all)
    local_norms = jnp.sum(prior_ensemble * prior_ensemble, axis=1)
    summed = lax.psum(local_norms, "space")
    particle_lengths = lax.all_gather(summed, "mem", axis=0, tiled=True)
    gaussian_variates = terminal_particles
    for step in range(ITERS):
        t = 1.0 - step / ITERS
        dt = 1.0 / ITERS
        alpha = 1.0 - 0.5 * t
        drift = -0.5 / alpha
        g2 = 1.0 + t / alpha
        damp = 1.0 - t
        partial_gram = jnp.einsum(
            "sv,mv->sm",
            gaussian_variates,
            particle_vectors,
            precision=peak_log_likelihood,
            preferred_element_type=jnp.float32,
        )
        inner_pairing_matrix = lax.psum(partial_gram, ("space", "mem"))
        annealed_importance = member_weights(
            inner_pairing_matrix, particle_lengths, alpha, t, temper
        )
        mixed_correction = jnp.dot(
            annealed_importance,
            particle_vectors,
            precision=peak_log_likelihood,
            preferred_element_type=jnp.float32,
        )
        score = -(gaussian_variates - alpha * mixed_correction) / t + damp * 4.0 * (
            measured_angles[None, :] - jnp.arctan(gaussian_variates)
        ) / (1.0 + gaussian_variates * gaussian_variates)
        gaussian_variates = (
            gaussian_variates
            + dt * (-drift * gaussian_variates + g2 * score)
            + math.sqrt(dt * g2) * reverse_perturbation[step]
        )
    return gaussian_variates


def solution(mesh):
    in_specs = (
        P("mem", "space"),
        P(None, ("space", "mem")),
        P(None, None, ("space", "mem")),
        P(("space", "mem")),
    )
    out_specs = P(None, ("space", "mem"))
    return jax.shard_map(
        per_device, mesh=mesh, in_specs=in_specs, out_specs=out_specs, check_vma=False
    )
```

profile of v0, /device:TPU:0, one launch (start us, length us, event | category | flops | bytes accessed | tf_op | source)
XLA Modules:
  0.0 456.9 jit_solution(2915807042031662705)
XLA Ops:
  6.5 0.0 all-reduce.5.cloned.1.call-start
  6.5 1.1 copy.8
  7.7 21.6 %all_to_all.19 = f32[64,8,256]{2,0,1:T(8,128)S(1)} all-to-all(f32[64,8,256]{2,0,1:T(8,128)S(1)} %bitcast.29), channel_id=1, replica_groups=mesh['space'=4,'mem'=8] {'mem'}, dimensions={1} | all-to-all | bytes 1048576 | tf_op jit(solution)/shard_map/all_to_all | solution.py:19
  29.3 0.0 copy-done.4
  29.3 2.1 fusion.1
  31.4 0.0 all-reduce.5.cloned.1.call-update
  31.4 0.0 copy-done
  31.4 0.0 all-reduce.7.cloned.1.call-start
  31.5 0.0 copy-done.8
  31.5 0.6 dynamic-slice
  32.7 0.1 multiply_reduce_fusion
  32.9 5.7 %psum.29 = f32[64]{0:T(128)S(1)} all-reduce(f32[64]{0:T(128)S(1)} %multiply_reduce_fusion), channel_id=1, replica_groups=mesh['space'=4,'mem'=8] {'space'}, use_global_device_ids=true, to_apply=%region_2.0 | all-reduce | flops 64 | bytes 512 | tf_op jit(solution)/shard_map/psum | solution.py:25
  38.5 0.2 dynamic-update-slice
  38.8 20.0 %all-reduce = f32[512]{0:T(512)S(1)} all-reduce(f32[512]{0:T(512)S(1)} %dynamic-update-slice), channel_id=1, replica_groups=mesh['space'=4,'mem'=8] {'mem'}, use_global_device_ids=true, to_apply=%add | all-reduce | flops 512 | bytes 4096
  58.8 102.5 %all-reduce.5.cloned.1.call-done = f32[512,512]{1,0:T(8,128)} async-done(((f32[512,512]{1,0:T(8,128)}), f32[512,512]{1,0:T(8,128)}) %all-reduce.5.cloned.1.call-update) | async-done | bytes 1048592 | tf_op jit(solution)/shard_map/psum | solution.py:42
  161.3 2.4 subtract_multiply_fusion.2
  163.7 3.7 online-softmax
  167.4 0.0 copy-done.6
  167.4 3.9 fusion
  171.3 0.0 all-reduce.7.cloned.1.call-update
  171.3 0.2 all-reduce.9.cloned.1.call-start
  171.6 129.5 %all-reduce.7.cloned.1.call-done = f32[512,512]{1,0:T(8,128)} async-done(((f32[512,512]{1,0:T(8,128)}), f32[512,512]{1,0:T(8,128)}) %all-reduce.7.cloned.1.call-update) | async-done | bytes 1048592 | tf_op jit(solution)/shard_map/psum | solution.py:42
  301.1 2.4 subtract_multiply_fusion.1
  303.5 3.6 online-softmax.1
  307.1 2.8 bitcast_add_fusion.1
  309.9 0.0 copy-done.2
  309.9 2.1 fusion.2
  312.0 0.0 all-reduce.9.cloned.1.call-update
  312.0 129.8 %all-reduce.9.cloned.1.call-done = f32[512,512]{1,0:T(8,128)} async-done(((f32[512,512]{1,0:T(8,128)}), f32[512,512]{1,0:T(8,128)}) %all-reduce.9.cloned.1.call-update) | async-done | bytes 1048592 | tf_op jit(solution)/shard_map/psum | solution.py:42
  441.8 2.4 subtract_multiply_fusion
  444.2 3.6 online-softmax.2
  447.7 2.7 bitcast_add_fusion
  (15 shorter events, 0.0 us)
Async XLA Ops:
  6.5 22.8 %copy-start.4 = (f32[512,256]{1,0:T(8,128)S(1)}, f32[512,256]{1,0:T(8,128)}, u32[]{:S(2)}) copy-start(f32[512,256]{1,0:T(8,128)} %param.5) | copy-start | bytes 1572868
  6.5 154.7 %all-reduce.5.cloned.1.call-start = ((), (), s32[]{:S(2)}) async-start(), calls=%async_computation.1 | async-start | bytes 2097152 | tf_op jit(solution)/shard_map/psum | solution.py:42
  29.3 2.1 copy-start
  29.3 2.2 copy-start.8
  29.3 3.4 copy-start.3
  31.4 269.7 %all-reduce.7.cloned.1.call-start = ((), (), s32[]{:S(2)}) async-start(), calls=%async_computation.2 | async-start | bytes 2097152 | tf_op jit(solution)/shard_map/psum | solution.py:42
  161.3 6.1 %copy-start.7 = (f32[256]{0:T(256)S(1)}, f32[256]{0:T(256)}, u32[]{:S(2)}) copy-start(f32[256]{0:T(256)} %param.7) | copy-start | bytes 3076
  163.7 3.7 copy-start.1
  163.7 3.7 copy-start.6
  171.3 270.4 %all-reduce.9.cloned.1.call-start = ((), (), s32[]{:S(2)}) async-start(), calls=%async_computation.3 | async-start | bytes 2097152 | tf_op jit(solution)/shard_map/psum | solution.py:42
  303.5 3.6 copy-start.5
  307.1 2.8 copy-start.2
Sparse Core Ops, SparseCore 0:
  31.5 129.6 all-reduce.4
  171.5 129.5 all-reduce.6
  312.1 129.6 all-reduce.8
where the time goes:
time: 457 us
  waiting for transfers between devices  362 us (79%)
  blocking collectives  47.3 us (10%)
  between operations  13.8 us (3%)
  other arithmetic  12.8 us (3%)
  Pallas kernels  10.9 us (2%)
  matrix products  8.05 us (2%)
    psum x3, waiting for transfers between devices, per_device(): inner_pairing_matrix = lax.psum(partial_gram, ('space', 'mem'))  362 us
    all_to_all x1, blocking collectives, per_device(): lax.all_to_all(prior_ensemble, 'mem', split_axis=1, concat_axis=0, tiled=...  21.6 us
    unnamed x1, blocking collectives  20 us
    unnamed x3, Pallas kernels  10.9 us
  transfers between devices with their start and end apart: 3, of which 3 were waited for; matrix products, arithmetic and copies ran while one was open for 0% of the time, Pallas kernels for 0%

commit v1 on v0

--- a/solution.py
+++ b/solution.py
@@ -39,7 +39,7 @@
             precision=peak_log_likelihood,
             preferred_element_type=jnp.float32,
         )
-        inner_pairing_matrix = lax.psum(partial_gram, ("space", "mem"))
+        inner_pairing_matrix = jnp.sum(lax.all_gather(partial_gram, ("space", "mem")), axis=0)
         annealed_importance = member_weights(
             inner_pairing_matrix, particle_lengths, alpha, t, temper
         )

time: 457 us -> 680 us (1.49)
  waiting for transfers between devices: 362 us -> 550 us
  other arithmetic: 12.8 us -> 45.9 us
    all_gather x0 -> x3, waiting for transfers between devices: none -> 550 us  [per_device(): lax.all_gather(partial_gram, ('space', 'mem'))]
    psum x3 -> x0, waiting for transfers between devices: 362 us -> none  [per_device(): inner_pairing_matrix = lax.psum(partial_gram, ('space', 'mem'))]
    reduce_sum x0 -> x3, other arithmetic: none -> 36.8 us  [per_device(): jnp.sum(lax.all_gather(partial_gram, ('space', 'mem')), axis=0)]
where the time goes in v1:
time: 680 us; the launch traced here: 679 us
  waiting for transfers between devices  550 us (81%)
  blocking collectives  48.3 us (7%)
  other arithmetic  45.9 us (7%)
  between operations  13.8 us (2%)
  Pallas kernels  10.9 us (2%)
  matrix products  7.91 us (1%)
    all_gather x3, waiting for transfers between devices, per_device(): lax.all_gather(partial_gram, ('space', 'mem'))  550 us
    reduce_sum x3, other arithmetic, per_device(): jnp.sum(lax.all_gather(partial_gram, ('space', 'mem')), axis=0)  36.8 us
    all_to_all x1, blocking collectives, per_device(): lax.all_to_all(prior_ensemble, 'mem', split_axis=1, concat_axis=0, tiled=...  21.6 us
    unnamed x1, blocking collectives  21 us
  transfers between devices with their start and end apart: 3, of which 3 were waited for; matrix products, arithmetic and copies ran while one was open for 0% of the time, Pallas kernels for 0%

profile of v1, /device:TPU:0, one launch (start us, length us, event | category | flops | bytes accessed | tf_op | source)
XLA Modules:
  0.0 679.3 jit_solution(8825237776649882494)
XLA Ops:
  6.5 1.1 copy.8
  7.7 21.6 %all_to_all.19 = f32[64,8,256]{2,0,1:T(8,128)S(1)} all-to-all(f32[64,8,256]{2,0,1:T(8,128)S(1)} %bitcast.35), channel_id=1, replica_groups=mesh['space'=4,'mem'=8] {'mem'}, dimensions={1} | all-to-all | bytes 1048576 | tf_op jit(solution)/shard_map/all_to_all | solution.py:19
  29.3 2.0 fusion.1
  31.4 0.0 all-gather.7.cloned.1.call-update
  31.4 0.0 all-gather.9.cloned.1.call-start
  31.4 0.6 dynamic-slice
  32.7 0.1 multiply_reduce_fusion
  32.8 5.7 psum.7
  38.5 0.2 dynamic-update-slice
  38.7 21.0 %all-reduce = f32[512]{0:T(512)S(1)} all-reduce(f32[512]{0:T(512)S(1)} %dynamic-update-slice), channel_id=1, replica_groups=mesh['space'=4,'mem'=8] {'mem'}, use_global_device_ids=true, to_apply=%add | all-reduce | flops 512 | bytes 4096
  59.8 165.2 %all-gather.7.cloned.1.call-done = f32[16384,512]{1,0:T(8,128)} async-done(((f32[512,512]{1,0:T(8,128)}), f32[16384,512]{1,0:T(8,128)}) %all-gather.7.cloned.1.call-update) | async-done | bytes 33554448 | tf_op jit(solution)/shard_map/all_gather | solution.py:42
  225.0 12.3 %reduce_sum.63 = f32[512,512]{1,0:T(8,128)S(1)} reduce(f32[32,512,512]{2,1,0:T(8,128)} %bitcast.25, f32[]{:T(128)} %constant.24.clone.1), dimensions={0}, to_apply=%region_0.0 | reduce | flops 8126464 | bytes 34603012 | tf_op jit(solution)/shard_map/reduce_sum | solution.py:42
  237.3 0.0 copy-start.7
  237.3 1.1 subtract_multiply_fusion.2
  238.4 3.7 online-softmax
  242.2 3.9 fusion
  246.0 0.0 all-gather.9.cloned.1.call-update
  246.1 0.2 all-gather.11.cloned.1.call-start
  246.3 192.3 %all-gather.9.cloned.1.call-done = f32[16384,512]{1,0:T(8,128)} async-done(((f32[512,512]{1,0:T(8,128)}), f32[16384,512]{1,0:T(8,128)}) %all-gather.9.cloned.1.call-update) | async-done | bytes 33554448 | tf_op jit(solution)/shard_map/all_gather | solution.py:42
  438.6 12.3 %reduce_sum.66 = f32[512,512]{1,0:T(8,128)S(1)} reduce(f32[32,512,512]{2,1,0:T(8,128)} %bitcast.26, f32[]{:T(128)} %constant.24.clone.1), dimensions={0}, to_apply=%region_5.0 | reduce | flops 8126464 | bytes 34603012 | tf_op jit(solution)/shard_map/reduce_sum | solution.py:42
  450.8 1.1 subtract_multiply_fusion.1
  452.0 3.6 online-softmax.1
  455.6 0.0 copy-done.5
  455.6 2.8 bitcast_add_fusion.1
  458.4 0.0 copy-done.2
  458.4 2.0 fusion.2
  460.4 0.0 all-gather.11.cloned.1.call-update
  460.4 192.5 %all-gather.11.cloned.1.call-done = f32[16384,512]{1,0:T(8,128)} async-done(((f32[512,512]{1,0:T(8,128)}), f32[16384,512]{1,0:T(8,128)}) %all-gather.11.cloned.1.call-update) | async-done | bytes 33554448 | tf_op jit(solution)/shard_map/all_gather | solution.py:42
  653.0 12.3 %reduce_sum.68 = f32[512,512]{1,0:T(8,128)S(1)} reduce(f32[32,512,512]{2,1,0:T(8,128)} %bitcast.27, f32[]{:T(128)} %constant.24.clone.1), dimensions={0}, to_apply=%region_8.0 | reduce | flops 8126464 | bytes 34603012 | tf_op jit(solution)/shard_map/reduce_sum | solution.py:42
  665.2 1.1 subtract_multiply_fusion
  666.4 3.6 online-softmax.2
  669.9 2.9 bitcast_add_fusion
  (18 shorter events, 0.0 us)
Async XLA Ops:
  6.5 22.8 %copy-start.4 = (f32[512,256]{1,0:T(8,128)S(1)}, f32[512,256]{1,0:T(8,128)}, u32[]{:S(2)}) copy-start(f32[512,256]{1,0:T(8,128)} %param.5) | copy-start | bytes 1572868
  6.5 218.5 %all-gather.7.cloned.1.call-start = ((), (), s32[]{:S(2)}) async-start(), calls=%async_computation.1 | async-start | bytes 34603008 | tf_op jit(solution)/shard_map/all_gather | solution.py:42
  29.3 2.1 copy-start
  29.3 2.1 copy-start.8
  29.3 3.4 copy-start.3
  31.4 407.2 %all-gather.9.cloned.1.call-start = ((), (), s32[]{:S(2)}) async-start(), calls=%async_computation.2 | async-start | bytes 34603008 | tf_op jit(solution)/shard_map/all_gather | solution.py:42
  237.3 4.8 copy-start.7
  238.4 3.7 copy-start.1
  238.4 3.7 copy-start.6
  246.1 406.9 %all-gather.11.cloned.1.call-start = ((), (), s32[]{:S(2)}) async-start(), calls=%async_computation.3 | async-start | bytes 34603008 | tf_op jit(solution)/shard_map/all_gather | solution.py:42
  452.0 3.6 copy-start.5
  455.6 2.8 copy-start.2
Sparse Core Ops, SparseCore 0:
  31.5 193.4 all-gather.6
  246.2 192.3 all-gather.8
  460.6 192.3 all-gather.10
